TPU v7x, 128 devices: a whole 4x4x4 slice. The times are simulated.
128 devices in a mesh: row: 8 (over x, z_lo), col: 16 (over y, z_hi, core).
Axes of the slice: x: 4, y: 4, z: 4 (z_hi: 2, z_lo: 2; z = z_hi * 2 + z_lo), core: 2. Of those that a mesh axis runs over, the one named last changes fastest.
Arguments:
- gate_pre: bfloat16 [2048, 26624], P('col', 'row'), may hold values from -6 to 6
- up_pre: bfloat16 [2048, 26624], P('col', 'row'), may hold values from -6 to 6
- residual: bfloat16 [2048, 16384], P('row', 'col'), may hold values from -6 to 6
- base_weight: bfloat16 [26624, 16384], P('row', 'col'), may hold values from -0.0390625 to 0.0390625
- perturb: bfloat16 [26624, 16384], P('row', 'col'), may hold values from -0.0390625 to 0.0390625
- exponents: int32 [208, 16384], P('row', 'col'), may hold values from -2 to 1
Outputs:
- plus_out: bfloat16 [2048, 16384], P('row', 'col')
- minus_out: bfloat16 [2048, 16384], P('row', 'col')
All inputs are finite; a program needn't handle non-finite values.
Results may differ from a plain program's by a relative error of at most 0.004.
Values may be sent and summed in bfloat16 or wider, within the bound.
A program may use at most 128 MiB of HBM per device.

v0:
```python
import jax
import jax.numpy as jnp
from jax import lax
from jax.sharding import Mesh
from jax.sharding import PartitionSpec as P

ROW = ("row_0", "row_1")
step_size = 0.25


def own_rows(so_far, axes):
    for axis in axes:
        so_far = lax.psum_scatter(so_far, axis, scatter_dimension=0, tiled=True)
    return so_far


def swiglu(gate_part, up_part):
    return (jax.nn.silu(gate_part.astype(jnp.float32)) * up_part.astype(jnp.float32)).astype(
        jnp.bfloat16
    )


def on_device(gate_pre, up_pre, residual, base_weight, perturb, exponents):
    hidden = lax.all_gather(swiglu(gate_pre, up_pre), "col", axis=0, tiled=True)
    group_size = base_weight.shape[0] // exponents.shape[0]
    factor = jnp.repeat(jnp.exp2(exponents.astype(jnp.float32)), group_size, axis=0)
    shift = step_size * factor * perturb.astype(jnp.float32)
    weight_full = base_weight.astype(jnp.float32)
    plus_weight = (weight_full + shift).astype(jnp.bfloat16)
    minus_weight = (weight_full - shift).astype(jnp.bfloat16)
    stream = residual.astype(jnp.float32)
    stacked = jnp.concatenate([plus_weight, minus_weight], axis=1)
    summed = own_rows(jnp.dot(hidden, stacked, preferred_element_type=jnp.float32), ROW)
    columns = base_weight.shape[1]
    plus_sum = summed[:, :columns]
    minus_sum = summed[:, columns:]
    plus_out = (stream + plus_sum).astype(jnp.bfloat16)
    minus_out = (stream + minus_sum).astype(jnp.bfloat16)
    return (plus_out, minus_out)


def solution(mesh):
    finer = Mesh(mesh.devices.reshape(4, 2, mesh.shape["col"]), ("row_0", "row_1", "col"))
    in_specs = (
        P("col", ROW),
        P("col", ROW),
        P(ROW, "col"),
        P(ROW, "col"),
        P(ROW, "col"),
        P(ROW, "col"),
    )
    out_specs = (P(ROW, "col"), P(ROW, "col"))
    return jax.shard_map(
        on_device, mesh=finer, in_specs=in_specs, out_specs=out_specs, check_vma=False
    )
```

profile of v0, /device:TPU:1, one launch (start us, length us, event | category | flops | bytes accessed | tf_op | source)
XLA Modules:
  0.0 360.9 jit_solution(1346917091632960387)
XLA Ops:
  7.2 0.0 all-gather.2.cloned.1.call-start
  7.2 2.8 fusion.10
  10.0 0.0 all-gather.2.cloned.1.call-update
  10.1 0.0 reduce-scatter.3.cloned.1.call-start
  10.1 0.9 exponential_multiply_fusion
  11.0 10.9 %fusion = (bf16[3328,1024]{1,0:T(8,128)(2,1)}, bf16[3328,1024]{1,0:T(8,128)(2,1)}) fusion(bf16[3328,1024]{1,0:T(8,128)(2,1)} %param.9, bf16[3328,1024]{1,0:T(8,128)(2,1)} %param.10, f32[26,1024]{1,0:T(8,128)S(1)} %exponential_multiply_fusion), kind=kLoop, calls=%fused_computation.2 | loop fusion | flops 23855104 | bytes 27369472 | tf_op jit(solution)/shard_map/convert_element_type | solution.py:29
  22.0 87.9 %all-gather.2.cloned.1.call-done = bf16[2048,3328]{1,0:T(8,128)(2,1)} async-done(((bf16[128,3328]{1,0:T(8,128)(2,1)}), bf16[2048,3328]{1,0:T(8,128)(2,1)}) %all-gather.2.cloned.1.call-update) | async-done | bytes 13631504 | tf_op jit(solution)/shard_map/all_gather | solution.py:24
  109.9 37.3 %fusion.2 = f32[2048,2048]{1,0:T(8,128)} fusion(bf16[2048,3328]{1,0:T(8,128)(2,1)} %all-gather.2.cloned.1.call-done, bf16[3328,1024]{1,0:T(8,128)(2,1)} %get-tuple-element.3, bf16[3328,1024]{1,0:T(8,128)(2,1)} %get-tuple-element.2), kind=kOutput, calls=%fused_computation.4 | convolution fusion | flops 27944550400 | bytes 44040192 | tf_op jit(solution)/shard_map/dot_general | solution.py:33
  147.2 0.0 copy-start
  147.2 0.0 reduce-scatter.3.cloned.1.call-update
  147.2 0.0 reduce-scatter.5.cloned.1.call-start
  147.2 145.2 %reduce-scatter.3.cloned.1.call-done = f32[512,2048]{1,0:T(8,128)} async-done(((f32[2048,2048]{1,0:T(8,128)}), f32[512,2048]{1,0:T(8,128)}) %reduce-scatter.3.cloned.1.call-update) | async-done | bytes 4194320 | tf_op jit(solution)/shard_map/reduce_scatter | solution.py:13
  292.4 0.0 reduce-scatter.5.cloned.1.call-update
  292.5 59.1 %reduce-scatter.5.cloned.1.call-done = f32[256,2048]{1,0:T(8,128)} async-done(((f32[512,2048]{1,0:T(8,128)}), f32[256,2048]{1,0:T(8,128)}) %reduce-scatter.5.cloned.1.call-update) | async-done | bytes 2097168 | tf_op jit(solution)/shard_map/reduce_scatter | solution.py:13
  351.6 0.0 copy-done
  351.6 2.8 fusion.12
Async XLA Ops:
  7.2 102.7 %all-gather.2.cloned.1.call-start = ((), (), s32[]{:S(2)}) async-start(), calls=%async_computation.2 | async-start | bytes 14483456 | tf_op jit(solution)/shard_map/all_gather | solution.py:24
  10.1 282.4 %reduce-scatter.3.cloned.1.call-start = ((), (), s32[]{:S(2)}) async-start(), calls=%async_computation.3 | async-start | bytes 20971520 | tf_op jit(solution)/shard_map/reduce_scatter | solution.py:13
  147.2 204.4 %copy-start = (bf16[256,1024]{1,0:T(8,128)(2,1)S(1)}, bf16[256,1024]{1,0:T(8,128)(2,1)}, u32[]{:S(2)}) copy-start(bf16[256,1024]{1,0:T(8,128)(2,1)} %param.8) | copy-start | bytes 1572868
  147.2 204.4 %reduce-scatter.5.cloned.1.call-start = ((), (), s32[]{:S(2)}) async-start(), calls=%async_computation.4 | async-start | bytes 6291456 | tf_op jit(solution)/shard_map/reduce_scatter | solution.py:13
Sparse Core Ops, SparseCore 0:
  10.4 99.4 all-gather.1
  147.3 145.0 reduce-scatter.2
  295.0 56.5 reduce-scatter.4
where the time goes:
time: 361 us
  waiting for transfers between devices  292 us (81%)
  matrix products  37.3 us (10%)
  other arithmetic  17.5 us (5%)
  between operations  13.7 us (4%)
    reduce_scatter x2, waiting for transfers between devices, own_rows(): so_far = lax.psum_scatter(so_far, axis, scatter_dimension=0, tiled=True)  204 us
    all_gather x1, waiting for transfers between devices, on_device(): hidden = lax.all_gather(swiglu(gate_pre, up_pre), 'col', axis=0, tiled=True)  87.9 us
    dot_general x1, matrix products, on_device(): jnp.dot(hidden, stacked, preferred_element_type=jnp.float32)  37.3 us
    convert_element_type x1, other arithmetic, on_device(): plus_weight = (weight_full + shift).astype(jnp.bfloat16)  10.9 us
  transfers between devices with their start and end apart: 3, of which 3 were waited for; matrix products, arithmetic and copies ran while one was open for 3% of the time, Pallas kernels for 0%

commit v1 on v0

--- a/solution.py
+++ b/solution.py
@@ -6,6 +6,13 @@
 
 ROW = ("row_0", "row_1")
 step_size = 0.25
+
+
+def swapped_in(value, axis, dim):
+    n_dev = lax.axis_size(axis)
+    pieces = jnp.stack([value for _ in range(n_dev)])
+    pieces = lax.all_to_all(pieces, axis, split_axis=0, concat_axis=0)
+    return jnp.concatenate(pieces, axis=dim)
 
 
 def own_rows(so_far, axes):
@@ -21,7 +28,7 @@
 
 
 def on_device(gate_pre, up_pre, residual, base_weight, perturb, exponents):
-    hidden = lax.all_gather(swiglu(gate_pre, up_pre), "col", axis=0, tiled=True)
+    hidden = swapped_in(swiglu(gate_pre, up_pre), "col", 0)
     group_size = base_weight.shape[0] // exponents.shape[0]
     factor = jnp.repeat(jnp.exp2(exponents.astype(jnp.float32)), group_size, axis=0)
     shift = step_size * factor * perturb.astype(jnp.float32)

time: 361 us -> 499 us (1.38)
  waiting for transfers between devices: 292 us -> 416 us
  starting transfers between devices: 0.12 us -> 9.51 us
  local copies, waits for them, and re-layouts: 0.01 us -> 6.19 us
    all_to_all x0 -> x1, waiting for transfers between devices: none -> 207 us  [swapped_in(): pieces = lax.all_to_all(pieces, axis, split_axis=0, concat_axis=0)]
    all_gather x1 -> x0, waiting for transfers between devices: 87.9 us -> none  [on_device(): hidden = lax.all_gather(swiglu(gate_pre, up_pre), 'col', axis=0, tiled=True)]
    all_to_all x0 -> x1, starting transfers between devices: none -> 9.43 us  [swapped_in(): pieces = lax.all_to_all(pieces, axis, split_axis=0, concat_axis=0)]
    another operation x0 -> x1, local copies, waits for them, and re-layouts: none -> 6.19 us  [swapped_in(): pieces = jnp.stack([value for _ in range(n_dev)])]
  transfers between devices with their start and end apart: 3 -> 3, of which waited for: 3 -> 3; matrix products, arithmetic and copies ran while one was open for 3% -> 2% of each run, Pallas kernels for 0% -> 0%
where the time goes in v1:
time: 499 us
  waiting for transfers between devices  416 us (83%)
  matrix products  37.3 us (7%)
  other arithmetic  15.7 us (3%)
  between operations  14.1 us (3%)
  starting transfers between devices  9.51 us (2%)
  local copies, waits for them, and re-layouts  6.19 us (1%)
    reduce_scatter x2, waiting for transfers between devices, own_rows(): so_far = lax.psum_scatter(so_far, axis, scatter_dimension=0, tiled=True)  209 us
    all_to_all x1, waiting for transfers between devices, swapped_in(): pieces = lax.all_to_all(pieces, axis, split_axis=0, concat_axis=0)  207 us
    dot_general x1, matrix products, on_device(): jnp.dot(hidden, stacked, preferred_element_type=jnp.float32)  37.3 us
    convert_element_type x1, other arithmetic, on_device(): plus_weight = (weight_full + shift).astype(jnp.bfloat16)  10.9 us
  transfers between devices with their start and end apart: 3, of which 3 were waited for; matrix products, arithmetic and copies ran while one was open for 2% of the time, Pallas kernels for 0%

profile of v1, /device:TPU:1, one launch (start us, length us, event | category | flops | bytes accessed | tf_op | source)
XLA Modules:
  0.0 499.1 jit_solution(5914977842809859964)
XLA Ops:
  7.2 1.9 fusion.10
  9.1 6.2 %stack.2 = bf16[16,128,3328]{2,1,0:T(8,128)(2,1)} broadcast(bf16[128,3328]{1,0:T(8,128)(2,1)S(1)} %fusion.10), dimensions={1,2} | broadcast | bytes 14483456 | tf_op jit(solution)/shard_map/stack | solution.py:13
  15.3 0.0 copy-start.1
  15.3 9.4 %all-to-all-start = ((bf16[16,128,3328]{2,1,0:T(8,128)(2,1)}), bf16[16,128,3328]{2,1,0:T(8,128)(2,1)}, u32[]{:S(2)}, u32[]{:S(2)}) async-start(bf16[16,128,3328]{2,1,0:T(8,128)(2,1)} %stack.2), calls=%async_computation | async-start | bytes 27262976 | tf_op jit(solution)/shard_map/all_to_all | solution.py:14
  24.7 0.0 reduce-scatter.3.cloned.1.call-start
  24.8 0.0 copy-done.1
  24.8 10.9 %fusion = (bf16[3328,1024]{1,0:T(8,128)(2,1)}, bf16[3328,1024]{1,0:T(8,128)(2,1)}) fusion(bf16[3328,1024]{1,0:T(8,128)(2,1)} %param.9, bf16[3328,1024]{1,0:T(8,128)(2,1)} %param.10, f32[26,1024]{1,0:T(8,128)S(1)} %exponential_multiply_fusion), kind=kLoop, calls=%fused_computation.2 | loop fusion | flops 23855104 | bytes 27369472 | tf_op jit(solution)/shard_map/convert_element_type | solution.py:36
  35.7 207.0 %all-to-all-done = bf16[16,128,3328]{2,1,0:T(8,128)(2,1)} async-done(((bf16[16,128,3328]{2,1,0:T(8,128)(2,1)}), bf16[16,128,3328]{2,1,0:T(8,128)(2,1)}, u32[]{:S(2)}, u32[]{:S(2)}) %all-to-all-start) | async-done | bytes 13631520 | tf_op jit(solution)/shard_map/all_to_all | solution.py:14
  242.8 37.3 %fusion.2 = f32[2048,2048]{1,0:T(8,128)} fusion(bf16[2048,3328]{1,0:T(8,128)(2,1)} %bitcast, bf16[3328,1024]{1,0:T(8,128)(2,1)} %get-tuple-element.3, bf16[3328,1024]{1,0:T(8,128)(2,1)} %get-tuple-element.2), kind=kOutput, calls=%fused_computation.4 | convolution fusion | flops 27944550400 | bytes 44040192 | tf_op jit(solution)/shard_map/dot_general | solution.py:40
  280.0 0.0 copy-start
  280.0 0.0 reduce-scatter.3.cloned.1.call-update
  280.0 0.0 reduce-scatter.5.cloned.1.call-start
  280.1 150.1 %reduce-scatter.3.cloned.1.call-done = f32[512,2048]{1,0:T(8,128)} async-done(((f32[2048,2048]{1,0:T(8,128)}), f32[512,2048]{1,0:T(8,128)}) %reduce-scatter.3.cloned.1.call-update) | async-done | bytes 4194320 | tf_op jit(solution)/shard_map/reduce_scatter | solution.py:20
  430.2 0.0 reduce-scatter.5.cloned.1.call-update
  430.2 59.1 %reduce-scatter.5.cloned.1.call-done = f32[256,2048]{1,0:T(8,128)} async-done(((f32[512,2048]{1,0:T(8,128)}), f32[256,2048]{1,0:T(8,128)}) %reduce-scatter.5.cloned.1.call-update) | async-done | bytes 2097168 | tf_op jit(solution)/shard_map/reduce_scatter | solution.py:20
  489.4 0.0 copy-done
  489.4 2.8 fusion.12
  (1 shorter events, 0.0 us)
Async XLA Ops:
  15.3 9.5 %copy-start.1 = (s32[26,1024]{1,0:T(8,128)S(1)}, s32[26,1024]{1,0:T(8,128)}, u32[]{:S(2)}) copy-start(s32[26,1024]{1,0:T(8,128)} %param.11) | copy-start | bytes 319492
  15.3 227.5 %all-to-all-start = ((bf16[16,128,3328]{2,1,0:T(8,128)(2,1)}), bf16[16,128,3328]{2,1,0:T(8,128)(2,1)}, u32[]{:S(2)}, u32[]{:S(2)}) async-start(bf16[16,128,3328]{2,1,0:T(8,128)(2,1)} %stack.2), calls=%async_computation | async-start | bytes 27262976 | tf_op jit(solution)/shard_map/all_to_all | solution.py:14
  24.7 405.5 %reduce-scatter.3.cloned.1.call-start = ((), (), s32[]{:S(2)}) async-start(), calls=%async_computation.3 | async-start | bytes 20971520 | tf_op jit(solution)/shard_map/reduce_scatter | solution.py:20
  280.0 209.4 %copy-start = (bf16[256,1024]{1,0:T(8,128)(2,1)S(1)}, bf16[256,1024]{1,0:T(8,128)(2,1)}, u32[]{:S(2)}) copy-start(bf16[256,1024]{1,0:T(8,128)(2,1)} %param.8) | copy-start | bytes 1572868
  280.0 209.3 %reduce-scatter.5.cloned.1.call-start = ((), (), s32[]{:S(2)}) async-start(), calls=%async_computation.4 | async-start | bytes 6291456 | tf_op jit(solution)/shard_map/reduce_scatter | solution.py:20
Sparse Core Ops, SparseCore 0:
  280.2 150.0 reduce-scatter.2
  432.7 56.5 reduce-scatter.4
